TPU v7x, 128 devices: a whole 4x4x4 slice. The times are simulated.
128 devices in a mesh: seq: 32 (over x, z_lo, y), head: 2 (over core), dp: 2 (over z_hi).
Axes of the slice: x: 4, y: 4, z: 4 (z_hi: 2, z_lo: 2; z = z_hi * 2 + z_lo), core: 2. Of those that a mesh axis runs over, the one named last changes fastest.
Arguments:
- queries: bfloat16 [16384, 2048], P(('dp', 'seq'), 'head'), parts along dimension 0, may hold values from -32 to 32
- keys: bfloat16 [16384, 2048], P(('dp', 'seq'), 'head'), parts along dimension 0, may hold values from -32 to 32
- values: bfloat16 [16384, 2048], P(('dp', 'seq'), 'head'), parts along dimension 0, may hold values from -6 to 6
- out_grad: bfloat16 [16384, 4096], P(('dp', 'seq')), parts along dimension 0, may hold values from -6 to 6
- proj_weight: bfloat16 [4096, 2048], P(None, 'head'), may hold values from -0.09375 to 0.09375
- layout: int32 [64, 12], replicated, may hold values from -1 to 63, as said below
Outputs:
- query_grad: bfloat16 [16384, 2048], P(('dp', 'seq'), 'head'), parts along dimension 0
- key_grad: bfloat16 [16384, 2048], P(('dp', 'seq'), 'head'), parts along dimension 0
- value_grad: bfloat16 [16384, 2048], P(('dp', 'seq'), 'head'), parts along dimension 0
- proj_grad: float32 [8192, 2048], P(('dp', 'seq'), 'head'), parts along dimension 0
There are 2 independent parts, one for each index of `dp`. A program takes and returns all parts, laid end to end along the dimension named above; an argument that names none is the same for every part. Nothing has to cross between parts.
Inputs may be any that keep to these rules, and one draw needn't show every extreme that they name: `layout`: row i lists, in increasing order, some of the blocks j < i - 7 whose remainder modulo 16 equals one offset, below 8 and shared by all rows (the last row lists all of them), then the blocks max(0, i - w + 1) to i for a window w of its own between 1 and 8, and ends with -1 in the unused entries; a row whose block follows a block of that remainder has w = 8.
All inputs are finite; a program needn't handle non-finite values.
Results may differ from a plain program's by a relative error of at most 0.03.
Values may be sent and summed in bfloat16 or wider, within the bound.
A program may use at most 192 MiB of HBM per device.

v0:
```python
import jax
import jax.numpy as jnp
from jax import lax
from jax.sharding import PartitionSpec as P

HD = 128
BLK = 128
LOCAL = 8
STRIDE = 16


def passed_along(block, axis, distance):
    devices = range(lax.axis_size(axis))
    route = [(i - distance, i) for i in devices if i - distance in devices]
    return lax.ppermute(block, axis, route)


def broadcast(array, axis, root):
    mine = lax.axis_index(axis) == root
    return lax.psum(jnp.where(mine, array, jnp.zeros_like(array)), axis)


def listed(table_row, block_ids):
    return jnp.any(table_row[None, :] == block_ids[:, None], axis=1) & (block_ids >= 0)


def local(queries, keys, values, out_grad, proj_weight, layout):
    tok_dev = queries.shape[0]
    width = queries.shape[1]
    heads_here = width // HD
    blocks_dev = tok_dev // BLK
    block_count = layout.shape[0]
    summary_count = block_count // STRIDE
    score_scale = HD ** (-0.5)
    first_block = lax.axis_index("seq") * blocks_dev
    offset_block = layout[block_count - 1, 0] % STRIDE
    reach_back = (LOCAL - 2) // blocks_dev + 1
    span_blocks = [
        min(blocks_dev, LOCAL - 1 - hop_index * blocks_dev) for hop_index in range(reach_back)
    ]
    attn_grad = jnp.dot(out_grad, proj_weight, preferred_element_type=jnp.float32).astype(
        jnp.bfloat16
    )
    near_keys = []
    near_values = []
    for distance in range(reach_back, 0, -1):
        rows_needed = span_blocks[distance - 1] * BLK
        moved_keys, moved_values = passed_along(
            (keys[tok_dev - rows_needed :], values[tok_dev - rows_needed :]), "seq", distance
        )
        near_keys.append(moved_keys)
        near_values.append(moved_values)
    pool_keys = jnp.concatenate(near_keys + [keys], axis=0).reshape(-1, heads_here, HD)
    pool_values = jnp.concatenate(near_values + [values], axis=0).reshape(-1, heads_here, HD)

    def fetch_summary(scan_state, summary_index):
        block_id = summary_index * STRIDE + offset_block
        start_row = block_id % blocks_dev * BLK
        owner_rank = block_id // blocks_dev
        piece_keys = lax.dynamic_slice_in_dim(keys, start_row, BLK, 0)
        piece_values = lax.dynamic_slice_in_dim(values, start_row, BLK, 0)
        received = (
            broadcast(piece_keys, "seq", owner_rank),
            broadcast(piece_values, "seq", owner_rank),
        )
        return (scan_state, received)

    ignored, fetched = lax.scan(fetch_summary, None, jnp.arange(summary_count, dtype=jnp.int32))
    far_keys = fetched[0].reshape(summary_count * BLK, heads_here, HD)
    far_values = fetched[1].reshape(summary_count * BLK, heads_here, HD)
    far_ids = jnp.arange(summary_count, dtype=jnp.int32) * STRIDE + offset_block
    query_blocks = queries.reshape(blocks_dev, BLK, heads_here, HD)
    grad_blocks = attn_grad.reshape(blocks_dev, BLK, heads_here, HD)
    window_offsets = jnp.arange(LOCAL, dtype=jnp.int32)
    causal_local = jnp.arange(LOCAL * BLK)[None, :] <= (LOCAL - 1) * BLK + jnp.arange(BLK)[:, None]

    def query_step(scan_state, local_block):
        query_rows = query_blocks[local_block]
        grad_rows = grad_blocks[local_block]
        block_id = first_block + local_block
        table_row = layout[block_id]
        window_key_rows = lax.dynamic_slice_in_dim(pool_keys, local_block * BLK, LOCAL * BLK, 0)
        window_value_rows = lax.dynamic_slice_in_dim(pool_values, local_block * BLK, LOCAL * BLK, 0)
        window_ids = block_id - (LOCAL - 1) + window_offsets
        plain_window = (window_ids % STRIDE != offset_block) | (window_ids == block_id)
        local_allowed = (
            causal_local & jnp.repeat(listed(table_row, window_ids) & plain_window, BLK)[None, :]
        )
        far_allowed = jnp.repeat(listed(table_row, far_ids) & (far_ids < block_id), BLK)[None, :]
        near_scores = (
            jnp.einsum(
                "ahd,chd->hac", query_rows, window_key_rows, preferred_element_type=jnp.float32
            )
            * score_scale
        )
        far_scores = (
            jnp.einsum("ahd,chd->hac", query_rows, far_keys, preferred_element_type=jnp.float32)
            * score_scale
        )
        near_scores = jnp.where(local_allowed[None], near_scores, -jnp.inf)
        far_scores = jnp.where(far_allowed[None], far_scores, -jnp.inf)
        row_top = jnp.maximum(jnp.max(near_scores, axis=-1), jnp.max(far_scores, axis=-1))[
            ..., None
        ]
        row_total = jnp.sum(jnp.exp(near_scores - row_top), axis=-1, keepdims=True) + jnp.sum(
            jnp.exp(far_scores - row_top), axis=-1, keepdims=True
        )
        log_total = row_top + jnp.log(row_total)
        near_probs = jnp.exp(near_scores - log_total)
        far_probs = jnp.exp(far_scores - log_total)
        near_low = near_probs.astype(jnp.bfloat16)
        far_low = far_probs.astype(jnp.bfloat16)
        out_rows = (
            jnp.einsum(
                "hac,chd->ahd", near_low, window_value_rows, preferred_element_type=jnp.float32
            )
            + jnp.einsum("hac,chd->ahd", far_low, far_values, preferred_element_type=jnp.float32)
        ).astype(jnp.bfloat16)
        delta_rows = jnp.transpose(
            jnp.sum(out_rows.astype(jnp.float32) * grad_rows.astype(jnp.float32), axis=-1)
        )[..., None]
        near_dprob = jnp.einsum(
            "ahd,chd->hac", grad_rows, window_value_rows, preferred_element_type=jnp.float32
        )
        far_dprob = jnp.einsum(
            "ahd,chd->hac", grad_rows, far_values, preferred_element_type=jnp.float32
        )
        near_dscore = (score_scale * near_probs * (near_dprob - delta_rows)).astype(jnp.bfloat16)
        far_dscore = (score_scale * far_probs * (far_dprob - delta_rows)).astype(jnp.bfloat16)
        query_grad_rows = (
            jnp.einsum(
                "hac,chd->ahd", near_dscore, window_key_rows, preferred_element_type=jnp.float32
            )
            + jnp.einsum("hac,chd->ahd", far_dscore, far_keys, preferred_element_type=jnp.float32)
        ).astype(jnp.bfloat16)
        far_key_grad = scan_state[0] + jnp.einsum(
            "hac,ahd->chd", far_dscore, query_rows, preferred_element_type=jnp.float32
        )
        far_value_grad = scan_state[1] + jnp.einsum(
            "hac,ahd->chd", far_low, grad_rows, preferred_element_type=jnp.float32
        )
        start_row = local_block * BLK
        old_keys = lax.dynamic_slice_in_dim(scan_state[2], start_row, LOCAL * BLK, 0)
        old_values = lax.dynamic_slice_in_dim(scan_state[3], start_row, LOCAL * BLK, 0)
        new_keys = old_keys + jnp.einsum(
            "hac,ahd->chd", near_dscore, query_rows, preferred_element_type=jnp.float32
        )
        new_values = old_values + jnp.einsum(
            "hac,ahd->chd", near_low, grad_rows, preferred_element_type=jnp.float32
        )
        pool_key_grad = lax.dynamic_update_slice_in_dim(scan_state[2], new_keys, start_row, 0)
        pool_value_grad = lax.dynamic_update_slice_in_dim(scan_state[3], new_values, start_row, 0)
        new_state = (far_key_grad, far_value_grad, pool_key_grad, pool_value_grad)
        return (new_state, (out_rows, query_grad_rows, log_total[..., 0], delta_rows[..., 0]))

    far_zeros = jnp.zeros((summary_count * BLK, heads_here, HD), jnp.float32)
    pool_zeros = jnp.zeros((pool_keys.shape[0], heads_here, HD), jnp.float32)
    init_state = (far_zeros, far_zeros, pool_zeros, pool_zeros)
    state_out, scanned = lax.scan(query_step, init_state, jnp.arange(blocks_dev, dtype=jnp.int32))
    out_blocks, query_parts, log_blocks, delta_blocks = scanned
    attn_out = out_blocks.reshape(tok_dev, width)
    query_grad = query_parts.reshape(tok_dev, width)
    own_ids = first_block + jnp.arange(blocks_dev, dtype=jnp.int32)
    is_summary = own_ids % STRIDE == offset_block
    summary_slot = jnp.minimum(own_ids // STRIDE, summary_count - 1)
    summed = lax.psum((state_out[0], state_out[1]), "seq")
    far_key_sum = summed[0].reshape(summary_count, BLK, width)
    far_value_sum = summed[1].reshape(summary_count, BLK, width)
    far_key_add = jnp.take(far_key_sum, summary_slot, axis=0)
    far_value_add = jnp.take(far_value_sum, summary_slot, axis=0)
    own_start = (LOCAL - 1) * BLK
    key_grad = state_out[2][own_start:]
    value_grad = state_out[3][own_start:]
    pool_start = 0
    for distance in range(reach_back, 0, -1):
        rows_needed = span_blocks[distance - 1] * BLK
        back_keys, back_values = passed_along(
            (
                state_out[2][pool_start : pool_start + rows_needed],
                state_out[3][pool_start : pool_start + rows_needed],
            ),
            "seq",
            -distance,
        )
        key_grad = key_grad.at[tok_dev - rows_needed :].add(back_keys)
        value_grad = value_grad.at[tok_dev - rows_needed :].add(back_values)
        pool_start = pool_start + rows_needed
    key_total = key_grad.reshape(blocks_dev, BLK, width) + jnp.where(
        is_summary[:, None, None], far_key_add, 0.0
    )
    value_total = value_grad.reshape(blocks_dev, BLK, width) + jnp.where(
        is_summary[:, None, None], far_value_add, 0.0
    )
    proj_grad = lax.psum_scatter(
        lax.dot_general(
            out_grad, attn_out, (((0,), (0,)), ((), ())), preferred_element_type=jnp.float32
        ),
        "seq",
        scatter_dimension=0,
        tiled=True,
    )
    key_out = key_total.reshape(tok_dev, width).astype(jnp.bfloat16)
    value_out = value_total.reshape(tok_dev, width).astype(jnp.bfloat16)
    return (query_grad, key_out, value_out, proj_grad)


def solution(mesh):
    return jax.shard_map(
        local,
        mesh=mesh,
        in_specs=(
            P(("dp", "seq"), "head"),
            P(("dp", "seq"), "head"),
            P(("dp", "seq"), "head"),
            P(("dp", "seq"), None),
            P(None, "head"),
            P(),
        ),
        out_specs=(
            P(("dp", "seq"), "head"),
            P(("dp", "seq"), "head"),
            P(("dp", "seq"), "head"),
            P(("dp", "seq"), "head"),
        ),
        check_vma=False,
    )
```

profile of v0, /device:TPU:0, one launch (start us, length us, event | category | flops | bytes accessed | tf_op | source)
XLA Modules:
  0.0 2074.4 jit_solution(11944361138026221976)
XLA Ops:
  10.2 5.8 collective-permute-start.1
  16.0 4.7 collective-permute-start.2
  20.7 2.9 collective-permute-start.3
  29.0 3.1 collective-permute-start.4
  37.1 6.6 fusion.40
  43.7 1255.1 %while.53 = (s32[]{:T(128)}, bf16[4,128,1024]{2,1,0:T(8,128)(2,1)}, bf16[4,128,1024]{2,1,0:T(8,128)(2,1)}, s32[4]{0:T(128)S(1)}, s32[]{:T(128)}, /*index=5*/bf16...) while((s32[]{:T(128)}, bf16[4,128,1024]{2,1,0:T(8,128)(2,1)}, ...), condition=%wide.region_3.4_spmd, body=%wide.region_0.3_spmd.sunk | while | flops 524319 | bytes 5243400 | solution.py:68
  45.9 308.6 %all-reduce.9.cloned.1.call-done = (bf16[1,128,1024]{2,1,0:T(8,128)(2,1)}, bf16[1,128,1024]{2,1,0:T(8,128)(2,1)}) async-done(((bf16[1,128,1024]{2,1,0:T(8,128)(2,1)}, bf16[1,128,1024]{2,1,0:T(8,128)(2,1)}), (bf16[1,128,1024]{2,1,0:T(8,128)(2,1)}, bf16[1,128,1024]{2,1,0:T(8,128)(2,1)})) %all-reduce.9.cloned.1.call-update) | async-done | bytes 524304 | tf_op jit(solution)/shard_map/while/body/eval_jaxpr/psum | solution.py:20
  359.9 308.3 %all-reduce.9.cloned.1.call-done = (bf16[1,128,1024]{2,1,0:T(8,128)(2,1)}, bf16[1,128,1024]{2,1,0:T(8,128)(2,1)}) async-done(((bf16[1,128,1024]{2,1,0:T(8,128)(2,1)}, bf16[1,128,1024]{2,1,0:T(8,128)(2,1)}), (bf16[1,128,1024]{2,1,0:T(8,128)(2,1)}, bf16[1,128,1024]{2,1,0:T(8,128)(2,1)})) %all-reduce.9.cloned.1.call-update) | async-done | bytes 524304 | tf_op jit(solution)/shard_map/while/body/eval_jaxpr/psum | solution.py:20
  673.7 308.3 %all-reduce.9.cloned.1.call-done = (bf16[1,128,1024]{2,1,0:T(8,128)(2,1)}, bf16[1,128,1024]{2,1,0:T(8,128)(2,1)}) async-done(((bf16[1,128,1024]{2,1,0:T(8,128)(2,1)}, bf16[1,128,1024]{2,1,0:T(8,128)(2,1)}), (bf16[1,128,1024]{2,1,0:T(8,128)(2,1)}, bf16[1,128,1024]{2,1,0:T(8,128)(2,1)})) %all-reduce.9.cloned.1.call-update) | async-done | bytes 524304 | tf_op jit(solution)/shard_map/while/body/eval_jaxpr/psum | solution.py:20
  987.5 308.0 %all-reduce.9.cloned.1.call-done = (bf16[1,128,1024]{2,1,0:T(8,128)(2,1)}, bf16[1,128,1024]{2,1,0:T(8,128)(2,1)}) async-done(((bf16[1,128,1024]{2,1,0:T(8,128)(2,1)}, bf16[1,128,1024]{2,1,0:T(8,128)(2,1)}), (bf16[1,128,1024]{2,1,0:T(8,128)(2,1)}, bf16[1,128,1024]{2,1,0:T(8,128)(2,1)})) %all-reduce.9.cloned.1.call-update) | async-done | bytes 524304 | tf_op jit(solution)/shard_map/while/body/eval_jaxpr/psum | solution.py:20
  1303.8 2.4 copy.99
  1306.2 2.8 collective-permute-start.5
  1312.7 3.4 collective-permute-start.7
  1327.2 4.4 copy.75
  1331.6 2.5 broadcast_in_dim.123
  1334.1 2.5 broadcast_in_dim.123.clone
  1336.6 88.2 %while.54 = (s32[]{:T(128)}, f32[512,8,128]{0,2,1:T(8,128)}, f32[512,8,128]{0,2,1:T(8,128)}, f32[1152,8,128]{0,2,1:T(8,128)}, f32[1152,8,128]{0,2,1:T(8,128)}, /...) while((s32[]{:T(128)}, f32[512,8,128]{0,2,1:T(8,128)}, ...), condition=%wide.region_12.13_spmd.clone.clone.clone, body=%wide.region_4.12_spmd.clone.clone.clone.sunk | while | flops 2451831296 | bytes 213504784 | solution.py:159
  1341.1 3.0 fusion.100
  1346.2 2.6 fusion.102
  1365.1 5.0 fusion.104
  1372.0 3.9 fusion.106
  1375.9 2.5 fusion.107
  1384.9 3.0 fusion.100
  1389.9 2.6 fusion.102
  1400.5 3.5 bitcast_add_fusion.6
  1409.4 5.1 fusion.104
  1416.4 3.9 fusion.106
  1420.3 2.5 fusion.107
  1424.8 2.9 reshape.422
  1427.7 2.9 copy.101
  1430.7 2.9 reshape.424
  1433.6 3.0 copy.103
  1437.6 8.1 convolution_bitcast_fusion.2
  1445.8 2.7 fusion.49
  1459.2 9.6 collective-permute-done.12
  1470.1 7.1 collective-permute-done.8
  1478.5 9.2 collective-permute-done.15
  1491.1 3.5 collective-permute-done.14
  1494.6 8.0 collective-permute-done.13
  1504.4 2.3 copy.102
  1507.8 23.1 %collective-permute-done.10 = f32[256,8,128]{0,2,1:T(8,128)} collective-permute-done((f32[256,8,128]{0,2,1:T(8,128)}, f32[256,8,128]{0,2,1:T(8,128)}, u32[]{:S(2)}, u32[]{:S(2)}) %collective-permute-start.10) | collective-permute-done | bytes 1048608 | tf_op jit(solution)/shard_map/ppermute | solution.py:15
  1530.9 72.0 %collective-permute-done.9 = f32[256,8,128]{0,2,1:T(8,128)} collective-permute-done((f32[256,8,128]{0,2,1:T(8,128)}, f32[256,8,128]{0,2,1:T(8,128)}, u32[]{:S(2)}, u32[]{:S(2)}) %collective-permute-start.9) | collective-permute-done | bytes 1048608 | tf_op jit(solution)/shard_map/ppermute | solution.py:15
  1602.9 2.5 add_add_fusion.1
  1606.9 2.3 copy.100
  1609.2 250.2 %all-reduce.7.cloned.1.call-done = (f32[4,128,1024]{2,1,0:T(8,128)}, f32[4,128,1024]{2,1,0:T(8,128)}) async-done(((f32[4,128,1024]{2,1,0:T(8,128)}, f32[4,128,1024]{2,1,0:T(8,128)}), (f32[4,128,1024]{2,1,0:T(8,128)}, f32[4,128,1024]{2,1,0:T(8,128)})) %all-reduce.7.cloned.1.call-update) | async-done | bytes 4194320 | tf_op jit(solution)/shard_map/psum | solution.py:166
  1861.5 3.2 gather_fusion
  1864.7 3.4 fusion.42
  1868.1 197.1 %reduce-scatter.2.cloned.1.call-done = f32[128,1024]{0,1:T(8,128)} async-done(((f32[4096,1024]{0,1:T(8,128)}), f32[128,1024]{0,1:T(8,128)}) %reduce-scatter.2.cloned.1.call-update) | async-done | bytes 524304 | tf_op jit(solution)/shard_map/reduce_scatter | solution.py:194
  (234 shorter events, 119.6 us)
Async XLA Ops:
  8.0 29.1 %copy-start = (bf16[256,4096]{1,0:T(8,128)(2,1)S(1)}, bf16[256,4096]{1,0:T(8,128)(2,1)}, u32[]{:S(2)}) copy-start(bf16[256,4096]{1,0:T(8,128)(2,1)} %param.43) | copy-start | bytes 6291460
  8.0 28.2 %copy-start.19 = (bf16[256,1024]{1,0:T(8,128)(2,1)S(1)}, bf16[256,1024]{1,0:T(8,128)(2,1)}, u32[]{:S(2)}) copy-start(bf16[256,1024]{1,0:T(8,128)(2,1)} %param.40) | copy-start | bytes 1572868
  10.2 1302.5 %collective-permute-start.1 = (bf16[256,1024]{0,1:T(8,128)(2,1)}, bf16[256,1024]{0,1:T(8,128)(2,1)}, u32[]{:S(2)}, u32[]{:S(2)}) collective-permute-start(bf16[256,1024]{0,1:T(8,128)(2,1)} %copy.69), channel_id=1, source_target_pairs={{0,12},{4,16},{8,20},{12,24},{16,28},{20,32},{24,36},{28,40},{32,4... | collective-permute-start | bytes 1572872 | tf_op jit(solution)/shard_map/ppermute | solution.py:15
  16.0 1302.0 %collective-permute-start.2 = (bf16[256,1024]{0,1:T(8,128)(2,1)}, bf16[256,1024]{0,1:T(8,128)(2,1)}, u32[]{:S(2)}, u32[]{:S(2)}) collective-permute-start(bf16[256,1024]{0,1:T(8,128)(2,1)} %copy.69), channel_id=1, source_target_pairs={{0,8},{4,12},{8,16},{12,20},{16,24},{20,28},{24,32},{28,36},{32,40... | collective-permute-start | bytes 1572872 | tf_op jit(solution)/shard_map/ppermute | solution.py:15
  20.7 1299.3 %collective-permute-start.3 = (bf16[256,1024]{0,1:T(8,128)(2,1)}, bf16[256,1024]{0,1:T(8,128)(2,1)}, u32[]{:S(2)}, u32[]{:S(2)}) collective-permute-start(bf16[256,1024]{0,1:T(8,128)(2,1)} %copy.69), channel_id=1, source_target_pairs={{0,4},{4,8},{8,12},{12,16},{16,20},{20,24},{24,28},{28,32},{32,36}... | collective-permute-start | bytes 1572872 | tf_op jit(solution)/shard_map/ppermute | solution.py:15
  25.3 1281.0 %collective-permute-start = (bf16[128,1024]{0,1:T(8,128)(2,1)}, bf16[128,1024]{0,1:T(8,128)(2,1)}, u32[]{:S(2)}, u32[]{:S(2)}) collective-permute-start(bf16[128,1024]{0,1:T(8,128)(2,1)} %slice.222), channel_id=1, source_target_pairs={{0,16},{4,20},{8,24},{12,28},{16,32},{20,36},{24,40},{28,44},{32,4... | collective-permute-start | bytes 786440 | tf_op jit(solution)/shard_map/ppermute | solution.py:15
  29.0 1281.7 %collective-permute-start.4 = (bf16[128,1024]{1,0:T(8,128)(2,1)}, bf16[128,1024]{1,0:T(8,128)(2,1)S(1)}, u32[]{:S(2)}, u32[]{:S(2)}) collective-permute-start(bf16[128,1024]{1,0:T(8,128)(2,1)} %slice.205), channel_id=1, source_target_pairs={{0,16},{4,20},{8,24},{12,28},{16,32},{20,36},{24,40},{28,44},{32,4... | collective-permute-start | bytes 786440 | tf_op jit(solution)/shard_map/ppermute | solution.py:15
  37.1 6.6 copy-start.12
  37.1 6.6 copy-start.13
  43.7 310.8 %all-reduce.9.cloned.1.call-start = ((), (), s32[]{:S(2)}) async-start(), calls=%async_computation.3 | async-start | bytes 1048576 | tf_op jit(solution)/shard_map/while/body/eval_jaxpr/psum | solution.py:20
  357.8 310.4 %all-reduce.9.cloned.1.call-start = ((), (), s32[]{:S(2)}) async-start(), calls=%async_computation.3 | async-start | bytes 1048576 | tf_op jit(solution)/shard_map/while/body/eval_jaxpr/psum | solution.py:20
  671.6 310.4 %all-reduce.9.cloned.1.call-start = ((), (), s32[]{:S(2)}) async-start(), calls=%async_computation.3 | async-start | bytes 1048576 | tf_op jit(solution)/shard_map/while/body/eval_jaxpr/psum | solution.py:20
  985.4 310.1 %all-reduce.9.cloned.1.call-start = ((), (), s32[]{:S(2)}) async-start(), calls=%async_computation.3 | async-start | bytes 1048576 | tf_op jit(solution)/shard_map/while/body/eval_jaxpr/psum | solution.py:20
  1298.9 560.5 %all-reduce.7.cloned.1.call-start = ((), (), s32[]{:S(2)}) async-start(), calls=%async_computation.2 | async-start | bytes 8388608 | tf_op jit(solution)/shard_map/psum | solution.py:166
  1298.9 3.7 copy-start.17
  1306.2 17.6 collective-permute-start.5
  1310.7 14.0 collective-permute-start.6
  1312.7 12.8 collective-permute-start.7
  1336.7 9.3 copy-start.22
  1345.0 8.7 copy-start.6
  1348.8 3.8 copy-start.3
  1348.8 3.8 copy-start.15
  1359.7 3.7 copy-start.16
  1363.4 6.7 slice-start
  1365.1 5.0 slice-start.1
  1371.9 3.9 copy-start.5
  1375.8 4.6 copy-start.23
  1380.4 9.3 copy-start.22
  1388.8 8.7 copy-start.6
  1392.6 3.8 copy-start.3
  1392.6 3.8 copy-start.15
  1404.0 3.7 copy-start.16
  1407.7 6.8 slice-start
  1409.4 5.1 slice-start.1
  1416.4 3.9 copy-start.5
  1420.3 4.6 copy-start.23
  1436.6 628.6 %reduce-scatter.2.cloned.1.call-start = ((), (), s32[]{:S(2)}) async-start(), calls=%async_computation.1 | async-start | bytes 17301504 | tf_op jit(solution)/shard_map/reduce_scatter | solution.py:194
  1445.8 11.6 slice-start.2
  1445.8 11.6 slice-start.3
  1448.5 39.2 %collective-permute-start.15 = (f32[256,8,128]{0,2,1:T(8,128)S(1)}, f32[256,8,128]{0,2,1:T(8,128)S(1)}, u32[]{:S(2)}, u32[]{:S(2)}) collective-permute-start(f32[256,8,128]{0,2,1:T(8,128)S(1)} %get-tuple-element.786), channel_id=1, source_target_pairs={{4,0},{8,4},{12,8},{16,12},{20,16},{24,20},{28,24},{32,28},{36,32}... | collective-permute-start | bytes 3145736 | tf_op jit(solution)/shard_map/ppermute | solution.py:15
  1450.9 17.9 collective-permute-start.12
  1453.3 23.9 %collective-permute-start.8 = (f32[128,8,128]{0,2,1:T(8,128)S(1)}, f32[128,8,128]{0,2,1:T(8,128)S(1)}, u32[]{:S(2)}, u32[]{:S(2)}) collective-permute-start(f32[128,8,128]{0,2,1:T(8,128)S(1)} %slice.208), channel_id=1, source_target_pairs={{16,0},{20,4},{24,8},{28,12},{32,16},{36,20},{40,24},{44,28},{48,3... | collective-permute-start | bytes 1572872 | tf_op jit(solution)/shard_map/ppermute | solution.py:15
  1454.6 40.0 %collective-permute-start.14 = (f32[256,8,128]{0,2,1:T(8,128)S(1)}, f32[256,8,128]{0,2,1:T(8,128)S(1)}, u32[]{:S(2)}, u32[]{:S(2)}) collective-permute-start(f32[256,8,128]{0,2,1:T(8,128)S(1)} %get-tuple-element.787), channel_id=1, source_target_pairs={{8,0},{12,4},{16,8},{20,12},{24,16},{28,20},{32,24},{36,28},{40,32... | collective-permute-start | bytes 3145736 | tf_op jit(solution)/shard_map/ppermute | solution.py:15
  1455.9 33.1 %copy-start.20 = (bf16[2,128,8,128]{3,2,1,0:T(8,128)(2,1)S(1)}, bf16[2,128,8,128]{3,2,1,0:T(8,128)(2,1)}, u32[]{:S(2)}) copy-start(bf16[2,128,8,128]{3,2,1,0:T(8,128)(2,1)} %get-tuple-element.496) | copy-start | bytes 1572868
  1455.9 46.7 %collective-permute-start.13 = (f32[256,8,128]{0,2,1:T(8,128)S(1)}, f32[256,8,128]{0,2,1:T(8,128)S(1)}, u32[]{:S(2)}, u32[]{:S(2)}) collective-permute-start(f32[256,8,128]{0,2,1:T(8,128)S(1)} %get-tuple-element.784), channel_id=1, source_target_pairs={{12,0},{16,4},{20,8},{24,12},{28,16},{32,20},{36,24},{40,28},{44,3... | collective-permute-start | bytes 3145736 | tf_op jit(solution)/shard_map/ppermute | solution.py:15
  1468.8 39.0 %collective-permute-start.11 = (f32[256,8,128]{0,2,1:T(8,128)}, f32[256,8,128]{0,2,1:T(8,128)}, u32[]{:S(2)}, u32[]{:S(2)}) collective-permute-start(f32[256,8,128]{0,2,1:T(8,128)} %get-tuple-element.790), channel_id=1, source_target_pairs={{4,0},{8,4},{12,8},{16,12},{20,16},{24,20},{28,24},{32,28},{36,32}... | collective-permute-start | bytes 3145736 | tf_op jit(solution)/shard_map/ppermute | solution.py:15
  1477.2 53.7 %collective-permute-start.10 = (f32[256,8,128]{0,2,1:T(8,128)}, f32[256,8,128]{0,2,1:T(8,128)}, u32[]{:S(2)}, u32[]{:S(2)}) collective-permute-start(f32[256,8,128]{0,2,1:T(8,128)} %get-tuple-element.791), channel_id=1, source_target_pairs={{8,0},{12,4},{16,8},{20,12},{24,16},{28,20},{32,24},{36,28},{40,32... | collective-permute-start | bytes 3145736 | tf_op jit(solution)/shard_map/ppermute | solution.py:15
  1487.7 115.2 %collective-permute-start.9 = (f32[256,8,128]{0,2,1:T(8,128)}, f32[256,8,128]{0,2,1:T(8,128)}, u32[]{:S(2)}, u32[]{:S(2)}) collective-permute-start(f32[256,8,128]{0,2,1:T(8,128)} %get-tuple-element.788), channel_id=1, source_target_pairs={{12,0},{16,4},{20,8},{24,12},{28,16},{32,20},{36,24},{40,28},{44,3... | collective-permute-start | bytes 3145736 | tf_op jit(solution)/shard_map/ppermute | solution.py:15
  (19 other events, 49.1 us)
Sparse Core Ops, SparseCore 0:
  47.1 307.3 all-reduce.8
  361.2 307.0 all-reduce.8
  674.9 307.0 all-reduce.8
  988.4 307.0 all-reduce.8
Sparse Core Ops, SparseCore 1:
  1436.7 422.6 all-reduce.6
  1861.6 203.6 reduce-scatter.1
where the time goes:
time: 2080 us; the launch traced here: 2070 us
  waiting for transfers between devices  1810 us (87%)
  local copies, waits for them, and re-layouts  110 us (5%)
  matrix products  70.8 us (3%)
  starting transfers between devices  36.6 us (2%)
    psum x4, waiting for transfers between devices, broadcast(): return lax.psum(jnp.where(mine, array, jnp.zeros_like(array)), axis)  1230 us
    psum x1, waiting for transfers between devices, local(): summed = lax.psum((state_out[0], state_out[1]), 'seq')  250 us
    reduce_scatter x1, waiting for transfers between devices, local(): lax.psum_scatter(lax.dot_general(out_grad, attn_out, (((0,), (0,)), ((),...  197 us
    ppermute x16, waiting for transfers between devices, passed_along(): return lax.ppermute(block, axis, route)  134 us
  transfers between devices with their start and end apart: 22, of which 14 were waited for; matrix products, arithmetic and copies ran while one was open for 4% of the time, Pallas kernels for 0%

commit v1 on v0

--- a/solution.py
+++ b/solution.py
@@ -17,7 +17,7 @@
 
 def broadcast(array, axis, root):
     mine = lax.axis_index(axis) == root
-    return lax.psum(jnp.where(mine, array, jnp.zeros_like(array)), axis)
+    return jnp.sum(lax.all_gather(jnp.where(mine, array, jnp.zeros_like(array)), axis), axis=0)
 
 
 def listed(table_row, block_ids):

time: 2080 us -> 2200 us (1.058)
  waiting for transfers between devices: 1810 us -> 1900 us
  other arithmetic: 15.4 us -> 66.1 us
    all_gather x0 -> x8, waiting for transfers between devices: none -> 1320 us  [broadcast(): lax.all_gather(jnp.where(mine, array, jnp.zeros_like(array)), axis)]
    psum x4 -> x0, waiting for transfers between devices: 1230 us -> none  [broadcast(): return lax.psum(jnp.where(mine, array, jnp.zeros_like(array)), axis)]
    reduce_sum x0 -> x8, other arithmetic: none -> 44.4 us  [broadcast(): jnp.sum(lax.all_gather(jnp.where(mine, array, jnp.zeros_like(array)), axi...]
  transfers between devices with their start and end apart: 22 -> 26, of which waited for: 14 -> 17; matrix products, arithmetic and copies ran while one was open for 4% -> 6% of each run, Pallas kernels for 0% -> 0%
where the time goes in v1:
time: 2200 us
  waiting for transfers between devices  1900 us (86%)
  local copies, waits for them, and re-layouts  104 us (5%)
  matrix products  70.8 us (3%)
  other arithmetic  66.1 us (3%)
  starting transfers between devices  35.6 us (2%)
    all_gather x8, waiting for transfers between devices, broadcast(): lax.all_gather(jnp.where(mine, array, jnp.zeros_like(array)), axis)  1320 us
    psum x1, waiting for transfers between devices, local(): summed = lax.psum((state_out[0], state_out[1]), 'seq')  253 us
    reduce_scatter x1, waiting for transfers between devices, local(): lax.psum_scatter(lax.dot_general(out_grad, attn_out, (((0,), (0,)), ((),...  197 us
    ppermute x16, waiting for transfers between devices, passed_along(): return lax.ppermute(block, axis, route)  122 us
    reduce_sum x8, other arithmetic, broadcast(): jnp.sum(lax.all_gather(jnp.where(mine, array, jnp.zeros_like(array)), axi...  44.4 us
  transfers between devices with their start and end apart: 26, of which 17 were waited for; matrix products, arithmetic and copies ran while one was open for 6% of the time, Pallas kernels for 0%

profile of v1, /device:TPU:0, one launch (start us, length us, event | category | flops | bytes accessed | tf_op | source)
XLA Modules:
  0.0 2199.6 jit_solution(7132508916437035482)
XLA Ops:
  10.2 5.8 collective-permute-start.1
  16.0 4.7 collective-permute-start.2
  20.7 2.9 collective-permute-start.3
  29.0 3.1 collective-permute-start.4
  37.1 6.6 fusion.40
  43.7 1389.2 %while.54 = (s32[]{:T(128)}, bf16[4,128,1024]{2,1,0:T(8,128)(2,1)}, bf16[4,128,1024]{2,1,0:T(8,128)(2,1)}, s32[4]{0:T(128)S(1)}, s32[]{:T(128)}, /*index=5*/bf16...) while((s32[]{:T(128)}, bf16[4,128,1024]{2,1,0:T(8,128)(2,1)}, ...), condition=%wide.region_3.4_spmd, body=%wide.region_0.3_spmd.sunk | while | flops 8388639 | bytes 71303744 | solution.py:68
  47.6 166.8 %all-gather.9.cloned.1.call-done = bf16[4096,1024]{1,0:T(8,128)(2,1)} async-done(((bf16[128,1024]{1,0:T(8,128)(2,1)}), bf16[4096,1024]{1,0:T(8,128)(2,1)}) %all-gather.9.cloned.1.call-update) | async-done | bytes 8388624 | tf_op jit(solution)/shard_map/while/body/eval_jaxpr/all_gather | solution.py:20
  214.4 5.5 reduce_sum.77
  220.0 163.9 %all-gather.11.cloned.1.call-done = bf16[4096,1024]{1,0:T(8,128)(2,1)} async-done(((bf16[128,1024]{1,0:T(8,128)(2,1)}), bf16[4096,1024]{1,0:T(8,128)(2,1)}) %all-gather.11.cloned.1.call-update) | async-done | bytes 8388624 | tf_op jit(solution)/shard_map/while/body/eval_jaxpr/all_gather | solution.py:20
  383.9 5.5 reduce_sum.78
  394.7 167.1 %all-gather.9.cloned.1.call-done = bf16[4096,1024]{1,0:T(8,128)(2,1)} async-done(((bf16[128,1024]{1,0:T(8,128)(2,1)}), bf16[4096,1024]{1,0:T(8,128)(2,1)}) %all-gather.9.cloned.1.call-update) | async-done | bytes 8388624 | tf_op jit(solution)/shard_map/while/body/eval_jaxpr/all_gather | solution.py:20
  561.9 5.5 reduce_sum.77
  567.4 163.8 %all-gather.11.cloned.1.call-done = bf16[4096,1024]{1,0:T(8,128)(2,1)} async-done(((bf16[128,1024]{1,0:T(8,128)(2,1)}), bf16[4096,1024]{1,0:T(8,128)(2,1)}) %all-gather.11.cloned.1.call-update) | async-done | bytes 8388624 | tf_op jit(solution)/shard_map/while/body/eval_jaxpr/all_gather | solution.py:20
  731.2 5.5 reduce_sum.78
  742.0 167.1 %all-gather.9.cloned.1.call-done = bf16[4096,1024]{1,0:T(8,128)(2,1)} async-done(((bf16[128,1024]{1,0:T(8,128)(2,1)}), bf16[4096,1024]{1,0:T(8,128)(2,1)}) %all-gather.9.cloned.1.call-update) | async-done | bytes 8388624 | tf_op jit(solution)/shard_map/while/body/eval_jaxpr/all_gather | solution.py:20
  909.2 5.5 reduce_sum.77
  914.7 163.8 %all-gather.11.cloned.1.call-done = bf16[4096,1024]{1,0:T(8,128)(2,1)} async-done(((bf16[128,1024]{1,0:T(8,128)(2,1)}), bf16[4096,1024]{1,0:T(8,128)(2,1)}) %all-gather.11.cloned.1.call-update) | async-done | bytes 8388624 | tf_op jit(solution)/shard_map/while/body/eval_jaxpr/all_gather | solution.py:20
  1078.5 5.5 reduce_sum.78
  1089.4 167.1 %all-gather.9.cloned.1.call-done = bf16[4096,1024]{1,0:T(8,128)(2,1)} async-done(((bf16[128,1024]{1,0:T(8,128)(2,1)}), bf16[4096,1024]{1,0:T(8,128)(2,1)}) %all-gather.9.cloned.1.call-update) | async-done | bytes 8388624 | tf_op jit(solution)/shard_map/while/body/eval_jaxpr/all_gather | solution.py:20
  1256.5 5.5 reduce_sum.77
  1262.0 163.9 %all-gather.11.cloned.1.call-done = bf16[4096,1024]{1,0:T(8,128)(2,1)} async-done(((bf16[128,1024]{1,0:T(8,128)(2,1)}), bf16[4096,1024]{1,0:T(8,128)(2,1)}) %all-gather.11.cloned.1.call-update) | async-done | bytes 8388624 | tf_op jit(solution)/shard_map/while/body/eval_jaxpr/all_gather | solution.py:20
  1425.9 5.5 reduce_sum.78
  1445.5 3.7 collective-permute-start.7
  1460.2 4.4 copy.75
  1469.7 88.2 %while.55 = (s32[]{:T(128)}, f32[512,8,128]{0,2,1:T(8,128)}, f32[512,8,128]{0,2,1:T(8,128)}, f32[1152,8,128]{0,2,1:T(8,128)}, f32[1152,8,128]{0,2,1:T(8,128)}, /...) while((s32[]{:T(128)}, f32[512,8,128]{0,2,1:T(8,128)}, ...), condition=%wide.region_12.13_spmd.clone.clone.clone, body=%wide.region_4.12_spmd.clone.clone.clone.sunk | while | flops 2451831296 | bytes 213504784 | solution.py:159
  1474.1 3.0 fusion.100
  1498.2 5.0 fusion.104
  1505.0 3.9 fusion.106
  1517.9 3.0 fusion.100
  1533.5 3.5 bitcast_add_fusion.6
  1542.6 5.0 fusion.104
  1549.4 3.9 fusion.106
  1557.9 2.9 reshape.424
  1560.8 2.9 copy.101
  1563.7 2.9 reshape.426
  1566.7 3.0 copy.103
  1570.7 8.1 convolution_bitcast_fusion.2
  1592.2 9.1 collective-permute-done.12
  1602.6 7.1 collective-permute-done.8
  1611.0 12.6 collective-permute-done.15
  1628.1 4.9 collective-permute-done.13
  1637.1 6.7 collective-permute-done.11
  1643.8 21.7 collective-permute-done.10
  1665.5 59.5 %collective-permute-done.9 = f32[256,8,128]{0,2,1:T(8,128)} collective-permute-done((f32[256,8,128]{0,2,1:T(8,128)}, f32[256,8,128]{0,2,1:T(8,128)}, u32[]{:S(2)}, u32[]{:S(2)}) %collective-permute-start.9) | collective-permute-done | bytes 1048608 | tf_op jit(solution)/shard_map/ppermute | solution.py:15
  1731.3 253.1 %all-reduce.3.cloned.1.call-done = (f32[4,128,1024]{2,1,0:T(8,128)}, f32[4,128,1024]{2,1,0:T(8,128)}) async-done(((f32[4,128,1024]{2,1,0:T(8,128)}, f32[4,128,1024]{2,1,0:T(8,128)}), (f32[4,128,1024]{2,1,0:T(8,128)}, f32[4,128,1024]{2,1,0:T(8,128)})) %all-reduce.3.cloned.1.call-update) | async-done | bytes 4194320 | tf_op jit(solution)/shard_map/psum | solution.py:166
  1986.5 3.2 gather_fusion
  1989.7 3.4 fusion.42
  1993.1 197.1 %reduce-scatter.2.cloned.1.call-done = f32[128,1024]{0,1:T(8,128)} async-done(((f32[4096,1024]{0,1:T(8,128)}), f32[128,1024]{0,1:T(8,128)}) %reduce-scatter.2.cloned.1.call-update) | async-done | bytes 524304 | tf_op jit(solution)/shard_map/reduce_scatter | solution.py:194
  (256 shorter events, 147.4 us)
Async XLA Ops:
  8.0 29.1 %copy-start = (bf16[256,4096]{1,0:T(8,128)(2,1)S(1)}, bf16[256,4096]{1,0:T(8,128)(2,1)}, u32[]{:S(2)}) copy-start(bf16[256,4096]{1,0:T(8,128)(2,1)} %param.43) | copy-start | bytes 6291460
  8.0 28.2 %copy-start.18 = (bf16[256,1024]{1,0:T(8,128)(2,1)S(1)}, bf16[256,1024]{1,0:T(8,128)(2,1)}, u32[]{:S(2)}) copy-start(bf16[256,1024]{1,0:T(8,128)(2,1)} %param.40) | copy-start | bytes 1572868
  10.2 1435.3 %collective-permute-start.1 = (bf16[256,1024]{0,1:T(8,128)(2,1)}, bf16[256,1024]{0,1:T(8,128)(2,1)}, u32[]{:S(2)}, u32[]{:S(2)}) collective-permute-start(bf16[256,1024]{0,1:T(8,128)(2,1)} %copy.69), channel_id=1, source_target_pairs={{0,12},{4,16},{8,20},{12,24},{16,28},{20,32},{24,36},{28,40},{32,4... | collective-permute-start | bytes 1572872 | tf_op jit(solution)/shard_map/ppermute | solution.py:15
  16.0 1435.2 %collective-permute-start.2 = (bf16[256,1024]{0,1:T(8,128)(2,1)}, bf16[256,1024]{0,1:T(8,128)(2,1)}, u32[]{:S(2)}, u32[]{:S(2)}) collective-permute-start(bf16[256,1024]{0,1:T(8,128)(2,1)} %copy.69), channel_id=1, source_target_pairs={{0,8},{4,12},{8,16},{12,20},{16,24},{20,28},{24,32},{28,36},{32,40... | collective-permute-start | bytes 1572872 | tf_op jit(solution)/shard_map/ppermute | solution.py:15
  20.7 1432.4 %collective-permute-start.3 = (bf16[256,1024]{0,1:T(8,128)(2,1)}, bf16[256,1024]{0,1:T(8,128)(2,1)}, u32[]{:S(2)}, u32[]{:S(2)}) collective-permute-start(bf16[256,1024]{0,1:T(8,128)(2,1)} %copy.69), channel_id=1, source_target_pairs={{0,4},{4,8},{8,12},{12,16},{16,20},{20,24},{24,28},{28,32},{32,36}... | collective-permute-start | bytes 1572872 | tf_op jit(solution)/shard_map/ppermute | solution.py:15
  25.3 1415.1 %collective-permute-start = (bf16[128,1024]{0,1:T(8,128)(2,1)}, bf16[128,1024]{0,1:T(8,128)(2,1)}, u32[]{:S(2)}, u32[]{:S(2)}) collective-permute-start(bf16[128,1024]{0,1:T(8,128)(2,1)} %slice.222), channel_id=1, source_target_pairs={{0,16},{4,20},{8,24},{12,28},{16,32},{20,36},{24,40},{28,44},{32,4... | collective-permute-start | bytes 786440 | tf_op jit(solution)/shard_map/ppermute | solution.py:15
  29.0 1414.4 %collective-permute-start.4 = (bf16[128,1024]{1,0:T(8,128)(2,1)}, bf16[128,1024]{1,0:T(8,128)(2,1)S(1)}, u32[]{:S(2)}, u32[]{:S(2)}) collective-permute-start(bf16[128,1024]{1,0:T(8,128)(2,1)} %slice.205), channel_id=1, source_target_pairs={{0,16},{4,20},{8,24},{12,28},{16,32},{20,36},{24,40},{28,44},{32,4... | collective-permute-start | bytes 786440 | tf_op jit(solution)/shard_map/ppermute | solution.py:15
  37.1 6.6 copy-start.12
  43.7 170.7 %all-gather.9.cloned.1.call-start = ((), (), s32[]{:S(2)}) async-start(), calls=%async_computation.3 | async-start | bytes 8650752 | tf_op jit(solution)/shard_map/while/body/eval_jaxpr/all_gather | solution.py:20
  46.8 337.1 %all-gather.11.cloned.1.call-start = ((), (), s32[]{:S(2)}) async-start(), calls=%async_computation.4 | async-start | bytes 8650752 | tf_op jit(solution)/shard_map/while/body/eval_jaxpr/all_gather | solution.py:20
  390.9 171.0 %all-gather.9.cloned.1.call-start = ((), (), s32[]{:S(2)}) async-start(), calls=%async_computation.3 | async-start | bytes 8650752 | tf_op jit(solution)/shard_map/while/body/eval_jaxpr/all_gather | solution.py:20
  393.9 337.3 %all-gather.11.cloned.1.call-start = ((), (), s32[]{:S(2)}) async-start(), calls=%async_computation.4 | async-start | bytes 8650752 | tf_op jit(solution)/shard_map/while/body/eval_jaxpr/all_gather | solution.py:20
  738.2 171.0 %all-gather.9.cloned.1.call-start = ((), (), s32[]{:S(2)}) async-start(), calls=%async_computation.3 | async-start | bytes 8650752 | tf_op jit(solution)/shard_map/while/body/eval_jaxpr/all_gather | solution.py:20
  741.2 337.3 %all-gather.11.cloned.1.call-start = ((), (), s32[]{:S(2)}) async-start(), calls=%async_computation.4 | async-start | bytes 8650752 | tf_op jit(solution)/shard_map/while/body/eval_jaxpr/all_gather | solution.py:20
  1085.5 171.0 %all-gather.9.cloned.1.call-start = ((), (), s32[]{:S(2)}) async-start(), calls=%async_computation.3 | async-start | bytes 8650752 | tf_op jit(solution)/shard_map/while/body/eval_jaxpr/all_gather | solution.py:20
  1088.5 337.4 %all-gather.11.cloned.1.call-start = ((), (), s32[]{:S(2)}) async-start(), calls=%async_computation.4 | async-start | bytes 8650752 | tf_op jit(solution)/shard_map/while/body/eval_jaxpr/all_gather | solution.py:20
  1433.0 551.4 %all-reduce.3.cloned.1.call-start = ((), (), s32[]{:S(2)}) async-start(), calls=%async_computation.2 | async-start | bytes 8388608 | tf_op jit(solution)/shard_map/psum | solution.py:166
  1440.4 16.5 collective-permute-start.5
  1443.5 14.2 collective-permute-start.6
  1445.5 13.0 collective-permute-start.7
  1469.7 9.3 copy-start.21
  1478.1 8.7 copy-start.6
  1481.8 3.8 copy-start.3
  1481.9 3.8 copy-start.14
  1496.5 6.8 slice-start
  1498.2 5.0 slice-start.1
  1505.0 3.9 copy-start.5
  1508.9 4.6 copy-start.22
  1513.5 9.3 copy-start.21
  1521.9 8.7 copy-start.6
  1525.7 3.8 copy-start.3
  1525.7 3.8 copy-start.14
  1540.8 6.7 slice-start
  1542.5 5.0 slice-start.1
  1549.4 3.9 copy-start.5
  1553.3 4.6 copy-start.22
  1569.7 620.5 %reduce-scatter.2.cloned.1.call-start = ((), (), s32[]{:S(2)}) async-start(), calls=%async_computation.1 | async-start | bytes 17301504 | tf_op jit(solution)/shard_map/reduce_scatter | solution.py:194
  1578.8 11.6 slice-start.2
  1578.8 11.6 slice-start.3
  1581.6 42.1 %collective-permute-start.15 = (f32[256,8,128]{0,2,1:T(8,128)S(1)}, f32[256,8,128]{0,2,1:T(8,128)S(1)}, u32[]{:S(2)}, u32[]{:S(2)}) collective-permute-start(f32[256,8,128]{0,2,1:T(8,128)S(1)} %get-tuple-element.811), channel_id=1, source_target_pairs={{4,0},{8,4},{12,8},{16,12},{20,16},{24,20},{28,24},{32,28},{36,32}... | collective-permute-start | bytes 3145736 | tf_op jit(solution)/shard_map/ppermute | solution.py:15
  1584.0 17.4 collective-permute-start.12
  1586.3 23.4 %collective-permute-start.8 = (f32[128,8,128]{0,2,1:T(8,128)S(1)}, f32[128,8,128]{0,2,1:T(8,128)S(1)}, u32[]{:S(2)}, u32[]{:S(2)}) collective-permute-start(f32[128,8,128]{0,2,1:T(8,128)S(1)} %slice.208), channel_id=1, source_target_pairs={{16,0},{20,4},{24,8},{28,12},{32,16},{36,20},{40,24},{44,28},{48,3... | collective-permute-start | bytes 1572872 | tf_op jit(solution)/shard_map/ppermute | solution.py:15
  1587.7 39.4 %collective-permute-start.14 = (f32[256,8,128]{0,2,1:T(8,128)S(1)}, f32[256,8,128]{0,2,1:T(8,128)S(1)}, u32[]{:S(2)}, u32[]{:S(2)}) collective-permute-start(f32[256,8,128]{0,2,1:T(8,128)S(1)} %get-tuple-element.812), channel_id=1, source_target_pairs={{8,0},{12,4},{16,8},{20,12},{24,16},{28,20},{32,24},{36,28},{40,32... | collective-permute-start | bytes 3145736 | tf_op jit(solution)/shard_map/ppermute | solution.py:15
  1589.0 36.0 %copy-start.19 = (bf16[2,128,8,128]{3,2,1,0:T(8,128)(2,1)S(1)}, bf16[2,128,8,128]{3,2,1,0:T(8,128)(2,1)}, u32[]{:S(2)}) copy-start(bf16[2,128,8,128]{3,2,1,0:T(8,128)(2,1)} %get-tuple-element.525) | copy-start | bytes 1572868
  1589.0 44.0 %collective-permute-start.13 = (f32[256,8,128]{0,2,1:T(8,128)S(1)}, f32[256,8,128]{0,2,1:T(8,128)S(1)}, u32[]{:S(2)}, u32[]{:S(2)}) collective-permute-start(f32[256,8,128]{0,2,1:T(8,128)S(1)} %get-tuple-element.809), channel_id=1, source_target_pairs={{12,0},{16,4},{20,8},{24,12},{28,16},{32,20},{36,24},{40,28},{44,3... | collective-permute-start | bytes 3145736 | tf_op jit(solution)/shard_map/ppermute | solution.py:15
  1601.3 42.5 %collective-permute-start.11 = (f32[256,8,128]{0,2,1:T(8,128)}, f32[256,8,128]{0,2,1:T(8,128)}, u32[]{:S(2)}, u32[]{:S(2)}) collective-permute-start(f32[256,8,128]{0,2,1:T(8,128)} %get-tuple-element.815), channel_id=1, source_target_pairs={{4,0},{8,4},{12,8},{16,12},{20,16},{24,20},{28,24},{32,28},{36,32}... | collective-permute-start | bytes 3145736 | tf_op jit(solution)/shard_map/ppermute | solution.py:15
  1609.7 55.8 %collective-permute-start.10 = (f32[256,8,128]{0,2,1:T(8,128)}, f32[256,8,128]{0,2,1:T(8,128)}, u32[]{:S(2)}, u32[]{:S(2)}) collective-permute-start(f32[256,8,128]{0,2,1:T(8,128)} %get-tuple-element.816), channel_id=1, source_target_pairs={{8,0},{12,4},{16,8},{20,12},{24,16},{28,20},{32,24},{36,28},{40,32... | collective-permute-start | bytes 3145736 | tf_op jit(solution)/shard_map/ppermute | solution.py:15
  1623.6 101.4 %collective-permute-start.9 = (f32[256,8,128]{0,2,1:T(8,128)}, f32[256,8,128]{0,2,1:T(8,128)}, u32[]{:S(2)}, u32[]{:S(2)}) collective-permute-start(f32[256,8,128]{0,2,1:T(8,128)} %get-tuple-element.813), channel_id=1, source_target_pairs={{12,0},{16,4},{20,8},{24,12},{28,16},{32,20},{36,24},{40,28},{44,3... | collective-permute-start | bytes 3145736 | tf_op jit(solution)/shard_map/ppermute | solution.py:15
  (22 other events, 57.6 us)
Sparse Core Ops, SparseCore 0:
  46.9 167.5 all-gather.8
  216.1 167.7 all-gather.10
  394.0 167.7 all-gather.8
  563.4 167.7 all-gather.10
  741.3 167.7 all-gather.8
  910.7 167.7 all-gather.10
  1088.6 167.7 all-gather.8
  1258.1 167.7 all-gather.10
Sparse Core Ops, SparseCore 1:
  1569.7 414.5 all-reduce.2
  1986.6 203.5 reduce-scatter.1
